TPU v7x, 256 devices: a whole 4x4x8 slice. The times are simulated.
256 devices in a mesh: gx: 16 (over z, core), gy: 16 (over y, x).
Axes of the slice: x: 4, y: 4, z: 8, core: 2. Of those that a mesh axis runs over, the one named last changes fastest.
Arguments:
- populations: float32 [19, 8, 128, 2048], P(None, None, 'gy', 'gx'), may hold values from 0.49 to 22.2, as said below
- concentrations: float32 [3, 8, 128, 2048], P(None, None, 'gy', 'gx'), may hold values from 0.5 to 2
- potential: float32 [8, 128, 2048], P(None, 'gy', 'gx'), may hold values from -5 to 5
- solid_mask: int32 [8, 128, 2048], P(None, 'gy', 'gx'), may hold values 0 or 1
- surface_sign: int32 [8, 128, 2048], P(None, 'gy', 'gx'), may hold values from -1 to 1
Outputs:
- populations_new: float32 [19, 8, 128, 2048], P(None, None, 'gy', 'gx')
- concentrations_new: float32 [3, 8, 128, 2048], P(None, None, 'gy', 'gx')
- potential_new: float32 [8, 128, 2048], P(None, 'gy', 'gx')
Inputs may be any that keep to these rules, and one draw needn't show every extreme that they name: `populations`: every entry is positive, near 36 times the weight of its velocity times a density of order one. `solid_mask`: 1 marks a solid cell, 0 a fluid one. `surface_sign`: read only at solid cells.
All inputs are finite; a program needn't handle non-finite values. No bound on the sum of `solid_mask` on one device may be relied on, other than what follows from the above.
Results may differ from a plain program's by a relative error of at most 0.0018.
Values sent between devices are 32-bit elements; how exact they have to be, the bound alone decides.
No kernel may reach another device: no remote copies, remote signals or barrier semaphores. Data moves between devices by JAX's collectives and lax.ppermute only.
A program may use at most 64 MiB of HBM per device.

v0:
```python
import jax
import jax.numpy as jnp
import numpy as np
from jax import lax
from jax.sharding import PartitionSpec as P

STEPS = 4
CYCLES = 2
SSTEP = 4
lattice_velocity = (
    (0, 0, 0),
    (0, 0, 1),
    (0, 0, -1),
    (0, 1, 0),
    (0, -1, 0),
    (1, 0, 0),
    (-1, 0, 0),
    (0, 1, 1),
    (0, -1, -1),
    (0, 1, -1),
    (0, -1, 1),
    (1, 0, 1),
    (-1, 0, -1),
    (1, 0, -1),
    (-1, 0, 1),
    (1, 1, 0),
    (-1, -1, 0),
    (1, -1, 0),
    (-1, 1, 0),
)
opposite = (0, 2, 1, 4, 3, 6, 5, 8, 7, 10, 9, 12, 11, 14, 13, 16, 15, 18, 17)
lattice_weight = (1.0 / 3.0,) + (1.0 / 18.0,) * 6 + (1.0 / 36.0,) * 12
moving = (1, 2, 3, 4, 7, 8, 9, 10, 11, 12, 13, 14, 15, 16, 17, 18)
relax_time = 1.25
force_scale = 0.05
valences = (1.0, -1.0, 2.0)
diffusivity = (0.05, 0.07, 0.03)
diag_coef = 6.0001
surface_scale = 2.0


def padded_2(block, sides, width):
    for axis, dim in sides:
        count = lax.axis_size(axis)
        forward = [(i, i + 1) for i in range(count - 1)]
        forward.append((count - 1, 0))
        backward = [(target, source) for source, target in forward]
        low = lax.ppermute(
            lax.slice_in_dim(block, block.shape[dim] - width, None, axis=dim), axis, forward
        )
        high = lax.ppermute(lax.slice_in_dim(block, 0, width, axis=dim), axis, backward)
        block = jnp.concatenate([low, block, high], axis=dim)
    return block


def lattice_dot(direction, vector):
    running = None
    for axis_id in range(3):
        if direction[axis_id] != 0:
            addend = vector[axis_id] if direction[axis_id] > 0 else -vector[axis_id]
            running = addend if running is None else running + addend
    return running


def ion_charge(concentration):
    return (
        valences[0] * concentration[0]
        + valences[1] * concentration[1]
        + valences[2] * concentration[2]
    )


def collide_cells(fields, concentration, fluid_mask, efield):
    density = fields[0]
    for member in range(1, 19):
        density = density + fields[member]
    momentum = []
    for axis_id in range(3):
        running = None
        for member in range(19):
            sign_val = lattice_velocity[member][axis_id]
            if sign_val != 0:
                addend = fields[member] if sign_val > 0 else -fields[member]
                running = addend if running is None else running + addend
        momentum.append(running)
    charge = fluid_mask * ion_charge(concentration)
    forcing = [force_scale * charge * efield[axis_id] for axis_id in range(3)]
    velocity = [(momentum[axis_id] + 0.5 * forcing[axis_id]) / density for axis_id in range(3)]
    speed_sq = velocity[0] * velocity[0] + velocity[1] * velocity[1] + velocity[2] * velocity[2]
    work_rate = velocity[0] * forcing[0] + velocity[1] * forcing[1] + velocity[2] * forcing[2]
    relaxed = []
    for member in range(19):
        weight = lattice_weight[member]
        if member == 0:
            projected = jnp.zeros_like(density)
            along_force = jnp.zeros_like(density)
        else:
            projected = lattice_dot(lattice_velocity[member], velocity)
            along_force = lattice_dot(lattice_velocity[member], forcing)
        balance = (
            weight
            * density
            * (1.0 + 3.0 * projected + 4.5 * projected * projected - 1.5 * speed_sq)
        )
        source = weight * (3.0 * (along_force - work_rate) + 9.0 * projected * along_force)
        relaxed.append(
            fields[member]
            - (fields[member] - balance) / relax_time
            + (1.0 - 0.5 / relax_time) * source
        )
    return (relaxed, velocity)


def face_flux(low, high, pot_low, pot_high, vel_low, vel_high, opened):
    rates = jnp.array(diffusivity, jnp.float32).reshape(3, 1, 1, 1)
    drift = jnp.array(valences, jnp.float32).reshape(3, 1, 1, 1) * rates
    middle = 0.5 * (low + high)
    return opened * (
        -rates * (high - low)
        - drift * middle * (pot_high - pot_low)
        + 0.5 * (vel_low + vel_high) * middle
    )


def ion_step(concentration, velocity, potential, fluid_mask, ion_pad, pot_rim, fluid_rim):
    fluxes = face_flux(
        concentration,
        jnp.roll(concentration, -1, 1),
        potential,
        jnp.roll(potential, -1, 0),
        velocity[0],
        jnp.roll(velocity[0], -1, 0),
        fluid_mask * jnp.roll(fluid_mask, -1, 0),
    )
    running = fluxes - jnp.roll(fluxes, 1, 1)
    conc_in = ion_pad[:3, :, :, 1:-1]
    pot_in = pot_rim[:, :, 1:-1]
    vel_in = ion_pad[3, :, :, 1:-1]
    open_in = fluid_rim[:, :, 1:-1]
    fluxes = face_flux(
        conc_in[:, :, :-1],
        conc_in[:, :, 1:],
        pot_in[:, :-1],
        pot_in[:, 1:],
        vel_in[:, :-1],
        vel_in[:, 1:],
        open_in[:, :-1] * open_in[:, 1:],
    )
    running = running + (fluxes[:, :, 1:] - fluxes[:, :, :-1])
    conc_in = ion_pad[:3, :, 1:-1, :]
    pot_in = pot_rim[:, 1:-1, :]
    vel_in = ion_pad[4, :, 1:-1, :]
    open_in = fluid_rim[:, 1:-1, :]
    fluxes = face_flux(
        conc_in[..., :-1],
        conc_in[..., 1:],
        pot_in[..., :-1],
        pot_in[..., 1:],
        vel_in[..., :-1],
        vel_in[..., 1:],
        open_in[..., :-1] * open_in[..., 1:],
    )
    running = running + (fluxes[..., 1:] - fluxes[..., :-1])
    return concentration - running


def neighbor_sum(padded):
    core = padded[:, :, 1:-1, 1:-1]
    return (
        jnp.roll(core, -1, 1)
        + jnp.roll(core, 1, 1)
        + (padded[:, :, 2:, 1:-1] + padded[:, :, :-2, 1:-1])
        + (padded[:, :, 1:-1, 2:] + padded[:, :, 1:-1, :-2])
    )


def next_level(summed, previous):
    if previous is None:
        return -summed / 6.0
    return -summed / 3.0 - previous


def shift_table():
    order_m = 2 * SSTEP + 1
    coeffs = np.zeros((order_m, order_m), np.float32)
    for block_start in (0, SSTEP + 1):
        block_depth = SSTEP if block_start == 0 else SSTEP - 1
        for column in range(block_depth):
            coeffs[block_start + column, block_start + column] = diag_coef
            coeffs[block_start + column + 1, block_start + column] = 6.0 if column == 0 else 3.0
            if column > 0:
                coeffs[block_start + column - 1, block_start + column] = 3.0
    return coeffs


def krylov_steps(gram_matrix):
    order_m = 2 * SSTEP + 1
    highest = lax.Precision.HIGHEST
    coeffs = jnp.asarray(shift_table(), jnp.float32)
    search_co = jnp.zeros((order_m,), jnp.float32).at[0].set(1.0)
    resid_co = jnp.zeros((order_m,), jnp.float32).at[SSTEP + 1].set(1.0)
    sol_co = jnp.zeros((order_m,), jnp.float32)
    residual_sq = jnp.dot(
        resid_co, jnp.dot(gram_matrix, resid_co, precision=highest), precision=highest
    )
    for inner_id in range(SSTEP):
        image_co = jnp.dot(coeffs, search_co, precision=highest)
        step_len = residual_sq / jnp.dot(
            search_co, jnp.dot(gram_matrix, image_co, precision=highest), precision=highest
        )
        sol_co = sol_co + step_len * search_co
        resid_co = resid_co - step_len * image_co
        fresh_sq = jnp.dot(
            resid_co, jnp.dot(gram_matrix, resid_co, precision=highest), precision=highest
        )
        search_co = resid_co + fresh_sq / residual_sq * search_co
        residual_sq = fresh_sq
    return (sol_co, resid_co, search_co)


def local(populations, concentrations, potential, solid_mask, surface_sign):
    highest = lax.Precision.HIGHEST
    fluid_mask = 1.0 - solid_mask.astype(jnp.float32)
    rows_y = potential.shape[1]
    cols_x = potential.shape[2]
    rims = padded_2(jnp.stack([potential, fluid_mask]), (("gx", 3), ("gy", 2)), 1)
    pot_rim = rims[0]
    fluid_rim = rims[1]
    efield = [
        (jnp.roll(potential, 1, 0) - jnp.roll(potential, -1, 0)) * 0.5,
        (pot_rim[:, :-2, 1:-1] - pot_rim[:, 2:, 1:-1]) * 0.5,
        (pot_rim[:, 1:-1, :-2] - pot_rim[:, 1:-1, 2:]) * 0.5,
    ]
    source_open = []
    for member in range(19):
        offset = lattice_velocity[member]
        window = fluid_rim[
            :, 1 - offset[1] : 1 - offset[1] + rows_y, 1 - offset[2] : 1 - offset[2] + cols_x
        ]
        source_open.append(jnp.roll(window, offset[0], 0))
    fields = [populations[member] for member in range(19)]
    concentration = concentrations
    for time_step in range(STEPS):
        relaxed, velocity = collide_cells(fields, concentration, fluid_mask, efield)
        stacked = jnp.concatenate(
            [
                jnp.stack([relaxed[member] for member in moving]),
                concentration,
                jnp.stack([velocity[1], velocity[2]]),
            ]
        )
        lattice_pad = padded_2(stacked, (("gx", 3), ("gy", 2)), 1)
        ion_pad = lattice_pad[len(moving) :]
        arrived = []
        for member in range(19):
            offset = lattice_velocity[member]
            if member in moving:
                slot_id = moving.index(member)
                piece = lattice_pad[
                    slot_id,
                    :,
                    1 - offset[1] : 1 - offset[1] + rows_y,
                    1 - offset[2] : 1 - offset[2] + cols_x,
                ]
            else:
                piece = relaxed[member]
            arrived.append(jnp.roll(piece, offset[0], 0))
        updated = [
            jnp.where(
                fluid_mask > 0.5,
                jnp.where(source_open[member] > 0.5, arrived[member], relaxed[opposite[member]]),
                fields[member],
            )
            for member in range(19)
        ]
        concentration = ion_step(
            concentration, velocity, potential, fluid_mask, ion_pad, pot_rim, fluid_rim
        )
        fields = updated
    target = fluid_mask * ion_charge(concentration) + surface_scale * surface_sign.astype(
        jnp.float32
    ) * (1.0 - fluid_mask)
    solution = potential
    start_pad = padded_2(solution[None], (("gx", 3), ("gy", 2)), 1)
    residual = target - (diag_coef * solution - neighbor_sum(start_pad)[0])
    search = residual
    for cycle_id in range(CYCLES):
        p_levels = [search]
        r_levels = [residual]
        previous = None
        current = jnp.stack([search, residual])
        for level_id in range(SSTEP):
            if level_id == SSTEP - 1:
                current = current[:1]
            padded = padded_2(current, (("gx", 3), ("gy", 2)), 1)
            following = next_level(
                neighbor_sum(padded), None if level_id == 0 else previous[: current.shape[0]]
            )
            previous = current
            current = following
            p_levels.append(current[0])
            if current.shape[0] > 1:
                r_levels.append(current[1])
        basis = jnp.stack(p_levels + r_levels)
        local_gram = jnp.einsum("aijk,bijk->ab", basis, basis, precision=highest)
        gram_matrix = lax.psum(local_gram, ("gx", "gy"))
        sol_co, resid_co, search_co = krylov_steps(gram_matrix)
        solution = solution + jnp.tensordot(sol_co, basis, axes=1, precision=highest)
        residual = jnp.tensordot(resid_co, basis, axes=1, precision=highest)
        search = jnp.tensordot(search_co, basis, axes=1, precision=highest)
    return (jnp.stack(fields), concentration, solution)


def solution(mesh):
    placed = (
        P(None, None, "gy", "gx"),
        P(None, None, "gy", "gx"),
        P(None, "gy", "gx"),
        P(None, "gy", "gx"),
        P(None, "gy", "gx"),
    )
    return jax.shard_map(
        local,
        mesh=mesh,
        in_specs=placed,
        out_specs=(P(None, None, "gy", "gx"), P(None, None, "gy", "gx"), P(None, "gy", "gx")),
        check_vma=False,
    )
```

profile of v0, /device:TPU:1, one launch (start us, length us, event | category | flops | bytes accessed | tf_op | source)
XLA Modules:
  0.0 479.0 jit_solution(2040877553520355775)
XLA Ops:
  11.4 3.8 collective-permute-start.3
  32.1 3.3 collective-permute-start.5
  43.5 5.4 %collective-permute-start.7 = (f32[21,8,1,130]{3,2,1,0:T(1,128)S(1)}, f32[21,8,1,130]{3,2,1,0:T(1,128)S(1)}, u32[]{:S(2)}, u32[]{:S(2)}) collective-permute-start(f32[21,8,1,130]{3,2,1,0:T(1,128)S(1)} %get-tuple-element.347), channel_id=1, source_target_pairs={{1,0},{2,1},{3,2},{4,3},{5,4},{6,5},{7,6},{8,7},{9,8},{10,9},{11,1... | collective-permute-start | bytes 262088 | tf_op jit(solution)/shard_map/ppermute | solution.py:51
  79.4 5.8 %collective-permute-start.11 = (f32[21,8,1,130]{3,2,1,0:T(1,128)S(1)}, f32[21,8,1,130]{3,2,1,0:T(1,128)S(1)}, u32[]{:S(2)}, u32[]{:S(2)}) collective-permute-start(f32[21,8,1,130]{3,2,1,0:T(1,128)S(1)} %get-tuple-element.341), channel_id=1, source_target_pairs={{1,0},{2,1},{3,2},{4,3},{5,4},{6,5},{7,6},{8,7},{9,8},{10,9},{11,1... | collective-permute-start | bytes 262088 | tf_op jit(solution)/shard_map/ppermute | solution.py:51
  115.1 5.6 %collective-permute-start.15 = (f32[21,8,1,130]{3,2,1,0:T(1,128)S(1)}, f32[21,8,1,130]{3,2,1,0:T(1,128)S(1)}, u32[]{:S(2)}, u32[]{:S(2)}) collective-permute-start(f32[21,8,1,130]{3,2,1,0:T(1,128)S(1)} %get-tuple-element.335), channel_id=1, source_target_pairs={{1,0},{2,1},{3,2},{4,3},{5,4},{6,5},{7,6},{8,7},{9,8},{10,9},{11,1... | collective-permute-start | bytes 262088 | tf_op jit(solution)/shard_map/ppermute | solution.py:51
  141.5 3.2 collective-permute-start.17
  146.2 5.1 %collective-permute-start.22 = (f32[1,8,1,130]{3,2,1,0:T(1,128)}, f32[1,8,1,130]{3,2,1,0:T(1,128)}, u32[]{:S(2)}, u32[]{:S(2)}) collective-permute-start(f32[1,8,1,130]{3,2,1,0:T(1,128)} %get-tuple-element.428), channel_id=1, source_target_pairs={{1,0},{2,1},{3,2},{4,3},{5,4},{6,5},{7,6},{8,7},{9,8},{10,9},{11,1... | collective-permute-start | bytes 12488 | tf_op jit(solution)/shard_map/ppermute | solution.py:51
  156.5 4.8 %collective-permute-start.19 = (f32[21,8,1,130]{3,2,1,0:T(1,128)S(1)}, f32[21,8,1,130]{3,2,1,0:T(1,128)S(1)}, u32[]{:S(2)}, u32[]{:S(2)}) collective-permute-start(f32[21,8,1,130]{3,2,1,0:T(1,128)S(1)} %get-tuple-element.328), channel_id=1, source_target_pairs={{1,0},{2,1},{3,2},{4,3},{5,4},{6,5},{7,6},{8,7},{9,8},{10,9},{11,1... | collective-permute-start | bytes 262088 | tf_op jit(solution)/shard_map/ppermute | solution.py:51
  170.8 3.6 collective-permute-start.25
  184.3 5.2 %collective-permute-start.26 = (f32[2,8,1,130]{3,0,2,1:T(2,128)S(1)}, f32[2,8,1,130]{3,0,2,1:T(2,128)S(1)}, u32[]{:S(2)}, u32[]{:S(2)}) collective-permute-start(f32[2,8,1,130]{3,0,2,1:T(2,128)S(1)} %get-tuple-element.402), channel_id=1, source_target_pairs={{1,0},{2,1},{3,2},{4,3},{5,4},{6,5},{7,6},{8,7},{9,8},{10,9},{11,1... | collective-permute-start | bytes 24968 | tf_op jit(solution)/shard_map/ppermute | solution.py:51
  190.4 5.0 %collective-permute-done.27 = f32[2,8,1,130]{3,0,2,1:T(2,128)S(1)} collective-permute-done((f32[2,8,1,130]{3,0,2,1:T(2,128)S(1)}, f32[2,8,1,130]{3,0,2,1:T(2,128)S(1)}, u32[]{:S(2)}, u32[]{:S(2)}) %collective-permute-start.27) | collective-permute-done | bytes 8352 | tf_op jit(solution)/shard_map/ppermute | solution.py:48
  196.2 4.4 collective-permute-start.29
  204.5 3.1 collective-permute-done.31
  208.2 5.1 %collective-permute-start.33 = (f32[2,8,8,1]{3,0,2,1:T(2,128)S(1)}, f32[2,8,8,1]{3,0,2,1:T(2,128)S(1)}, u32[]{:S(2)}, u32[]{:S(2)}) collective-permute-start(f32[2,8,8,1]{3,0,2,1:T(2,128)S(1)} %get-tuple-element.487), channel_id=1, source_target_pairs={{16,0},{32,16},{48,32},{64,48},{80,64},{96,80},{112,96},{128,112},... | collective-permute-start | bytes 1544 | tf_op jit(solution)/shard_map/ppermute | solution.py:51
  217.4 3.3 collective-permute-done.35
  221.3 5.1 %collective-permute-start.37 = (f32[1,8,8,1]{3,0,2,1:T(1,128)S(1)}, f32[1,8,8,1]{3,0,2,1:T(1,128)S(1)}, u32[]{:S(2)}, u32[]{:S(2)}) collective-permute-start(f32[1,8,8,1]{3,0,2,1:T(1,128)S(1)} %get-tuple-element.481), channel_id=1, source_target_pairs={{16,0},{32,16},{48,32},{64,48},{80,64},{96,80},{112,96},{128,112},... | collective-permute-start | bytes 776 | tf_op jit(solution)/shard_map/ppermute | solution.py:51
  230.3 3.1 collective-permute-done.39
  235.1 78.9 %psum.14 = f32[9,9]{1,0:T(8,128)S(1)} all-reduce(f32[9,9]{1,0:T(8,128)S(1)} %convolution_bitcast_fusion.1), channel_id=1, replica_groups=mesh['gx'=16,'gy'=16] {'gx','gy'}, use_global_device_ids=true, to_apply=%region_0.1 | all-reduce | flops 81 | bytes 648 | tf_op jit(solution)/shard_map/psum | solution.py:306
  340.5 4.5 collective-permute-done.43
  353.8 3.4 collective-permute-done.47
  366.1 3.1 collective-permute-done.51
  370.8 4.2 collective-permute-start.53
  378.9 3.1 collective-permute-done.55
  383.7 77.5 %psum.15 = f32[9,9]{1,0:T(8,128)S(1)} all-reduce(f32[9,9]{1,0:T(8,128)S(1)} %convolution_bitcast_fusion), channel_id=1, replica_groups=mesh['gx'=16,'gy'=16] {'gx','gy'}, use_global_device_ids=true, to_apply=%region_1.2 | all-reduce | flops 81 | bytes 648 | tf_op jit(solution)/shard_map/psum | solution.py:306
  (948 shorter events, 203.9 us)
Async XLA Ops:
  2.4 7.5 %collective-permute-start = (f32[2,8,8,1]{3,2,1,0:T(8,128)S(1)}, f32[2,8,8,1]{3,2,1,0:T(8,128)S(1)}, u32[]{:S(2)}, u32[]{:S(2)}) collective-permute-start(f32[2,8,8,1]{3,2,1,0:T(8,128)S(1)} %get-tuple-element.495), channel_id=1, source_target_pairs={{0,16},{16,32},{32,48},{48,64},{64,80},{80,96},{96,112},{112,128},... | collective-permute-start | bytes 1544 | tf_op jit(solution)/shard_map/ppermute | solution.py:48
  6.4 138.3 %collective-permute-start.20 = (f32[1,8,8,1]{3,2,1,0:T(8,128)}, f32[1,8,8,1]{3,2,1,0:T(8,128)}, u32[]{:S(2)}, u32[]{:S(2)}) collective-permute-start(f32[1,8,8,1]{3,2,1,0:T(8,128)} %get-tuple-element.508), channel_id=1, source_target_pairs={{0,16},{16,32},{32,48},{48,64},{64,80},{80,96},{96,112},{112,128},... | collective-permute-start | bytes 776 | tf_op jit(solution)/shard_map/ppermute | solution.py:48
  7.9 136.8 %collective-permute-start.21 = (f32[1,8,8,1]{3,2,1,0:T(8,128)}, f32[1,8,8,1]{3,2,1,0:T(8,128)}, u32[]{:S(2)}, u32[]{:S(2)}) collective-permute-start(f32[1,8,8,1]{3,2,1,0:T(8,128)} %get-tuple-element.507), channel_id=1, source_target_pairs={{16,0},{32,16},{48,32},{64,48},{80,64},{96,80},{112,96},{128,112},... | collective-permute-start | bytes 776 | tf_op jit(solution)/shard_map/ppermute | solution.py:51
  30.9 8.9 %collective-permute-start.4 = (f32[21,8,8,1]{0,2,3,1:T(8,128)S(1)}, f32[21,8,8,1]{0,2,3,1:T(8,128)S(1)}, u32[]{:S(2)}, u32[]{:S(2)}) collective-permute-start(f32[21,8,8,1]{0,2,3,1:T(8,128)S(1)} %copy.34), channel_id=1, source_target_pairs={{0,16},{16,32},{32,48},{48,64},{64,80},{80,96},{96,112},{112,128},... | collective-permute-start | bytes 16136 | tf_op jit(solution)/shard_map/ppermute | solution.py:48
  32.1 8.4 %collective-permute-start.5 = (f32[21,8,8,1]{0,2,3,1:T(8,128)S(1)}, f32[21,8,8,1]{0,2,3,1:T(8,128)}, u32[]{:S(2)}, u32[]{:S(2)}) collective-permute-start(f32[21,8,8,1]{0,2,3,1:T(8,128)S(1)} %copy.36), channel_id=1, source_target_pairs={{16,0},{32,16},{48,32},{64,48},{80,64},{96,80},{112,96},{128,112},... | collective-permute-start | bytes 16136 | tf_op jit(solution)/shard_map/ppermute | solution.py:51
  43.4 7.9 %collective-permute-start.6 = (f32[21,8,1,130]{3,2,1,0:T(1,128)S(1)}, f32[21,8,1,130]{3,2,1,0:T(1,128)S(1)}, u32[]{:S(2)}, u32[]{:S(2)}) collective-permute-start(f32[21,8,1,130]{3,2,1,0:T(1,128)S(1)} %get-tuple-element.346), channel_id=1, source_target_pairs={{0,1},{1,2},{2,3},{3,4},{4,5},{5,6},{6,7},{7,8},{8,9},{9,10},{10,1... | collective-permute-start | bytes 262088 | tf_op jit(solution)/shard_map/ppermute | solution.py:48
  43.5 7.8 %collective-permute-start.7 = (f32[21,8,1,130]{3,2,1,0:T(1,128)S(1)}, f32[21,8,1,130]{3,2,1,0:T(1,128)S(1)}, u32[]{:S(2)}, u32[]{:S(2)}) collective-permute-start(f32[21,8,1,130]{3,2,1,0:T(1,128)S(1)} %get-tuple-element.347), channel_id=1, source_target_pairs={{1,0},{2,1},{3,2},{4,3},{5,4},{6,5},{7,6},{8,7},{9,8},{10,9},{11,1... | collective-permute-start | bytes 262088 | tf_op jit(solution)/shard_map/ppermute | solution.py:51
  69.0 7.5 %collective-permute-start.8 = (f32[21,8,8,1]{0,2,3,1:T(8,128)S(1)}, f32[21,8,8,1]{0,2,3,1:T(8,128)S(1)}, u32[]{:S(2)}, u32[]{:S(2)}) collective-permute-start(f32[21,8,8,1]{0,2,3,1:T(8,128)S(1)} %copy.40), channel_id=1, source_target_pairs={{0,16},{16,32},{32,48},{48,64},{64,80},{80,96},{96,112},{112,128},... | collective-permute-start | bytes 16136 | tf_op jit(solution)/shard_map/ppermute | solution.py:48
  70.3 6.9 %collective-permute-start.9 = (f32[21,8,8,1]{0,2,3,1:T(8,128)S(1)}, f32[21,8,8,1]{0,2,3,1:T(8,128)S(1)}, u32[]{:S(2)}, u32[]{:S(2)}) collective-permute-start(f32[21,8,8,1]{0,2,3,1:T(8,128)S(1)} %copy.42), channel_id=1, source_target_pairs={{16,0},{32,16},{48,32},{64,48},{80,64},{96,80},{112,96},{128,112},... | collective-permute-start | bytes 16136 | tf_op jit(solution)/shard_map/ppermute | solution.py:51
  79.4 8.2 %collective-permute-start.10 = (f32[21,8,1,130]{3,2,1,0:T(1,128)S(1)}, f32[21,8,1,130]{3,2,1,0:T(1,128)S(1)}, u32[]{:S(2)}, u32[]{:S(2)}) collective-permute-start(f32[21,8,1,130]{3,2,1,0:T(1,128)S(1)} %get-tuple-element.340), channel_id=1, source_target_pairs={{0,1},{1,2},{2,3},{3,4},{4,5},{5,6},{6,7},{7,8},{8,9},{9,10},{10,1... | collective-permute-start | bytes 262088 | tf_op jit(solution)/shard_map/ppermute | solution.py:48
  79.4 8.2 %collective-permute-start.11 = (f32[21,8,1,130]{3,2,1,0:T(1,128)S(1)}, f32[21,8,1,130]{3,2,1,0:T(1,128)S(1)}, u32[]{:S(2)}, u32[]{:S(2)}) collective-permute-start(f32[21,8,1,130]{3,2,1,0:T(1,128)S(1)} %get-tuple-element.341), channel_id=1, source_target_pairs={{1,0},{2,1},{3,2},{4,3},{5,4},{6,5},{7,6},{8,7},{9,8},{10,9},{11,1... | collective-permute-start | bytes 262088 | tf_op jit(solution)/shard_map/ppermute | solution.py:51
  104.7 7.4 %collective-permute-start.12 = (f32[21,8,8,1]{0,2,3,1:T(8,128)S(1)}, f32[21,8,8,1]{0,2,3,1:T(8,128)S(1)}, u32[]{:S(2)}, u32[]{:S(2)}) collective-permute-start(f32[21,8,8,1]{0,2,3,1:T(8,128)S(1)} %copy.46), channel_id=1, source_target_pairs={{0,16},{16,32},{32,48},{48,64},{64,80},{80,96},{96,112},{112,128},... | collective-permute-start | bytes 16136 | tf_op jit(solution)/shard_map/ppermute | solution.py:48
  106.0 6.9 %collective-permute-start.13 = (f32[21,8,8,1]{0,2,3,1:T(8,128)S(1)}, f32[21,8,8,1]{0,2,3,1:T(8,128)S(1)}, u32[]{:S(2)}, u32[]{:S(2)}) collective-permute-start(f32[21,8,8,1]{0,2,3,1:T(8,128)S(1)} %copy.48), channel_id=1, source_target_pairs={{16,0},{32,16},{48,32},{64,48},{80,64},{96,80},{112,96},{128,112},... | collective-permute-start | bytes 16136 | tf_op jit(solution)/shard_map/ppermute | solution.py:51
  115.0 8.4 %collective-permute-start.14 = (f32[21,8,1,130]{3,2,1,0:T(1,128)S(1)}, f32[21,8,1,130]{3,2,1,0:T(1,128)S(1)}, u32[]{:S(2)}, u32[]{:S(2)}) collective-permute-start(f32[21,8,1,130]{3,2,1,0:T(1,128)S(1)} %get-tuple-element.334), channel_id=1, source_target_pairs={{0,1},{1,2},{2,3},{3,4},{4,5},{5,6},{6,7},{7,8},{8,9},{9,10},{10,1... | collective-permute-start | bytes 262088 | tf_op jit(solution)/shard_map/ppermute | solution.py:48
  115.1 8.3 %collective-permute-start.15 = (f32[21,8,1,130]{3,2,1,0:T(1,128)S(1)}, f32[21,8,1,130]{3,2,1,0:T(1,128)S(1)}, u32[]{:S(2)}, u32[]{:S(2)}) collective-permute-start(f32[21,8,1,130]{3,2,1,0:T(1,128)S(1)} %get-tuple-element.335), channel_id=1, source_target_pairs={{1,0},{2,1},{3,2},{4,3},{5,4},{6,5},{7,6},{8,7},{9,8},{10,9},{11,1... | collective-permute-start | bytes 262088 | tf_op jit(solution)/shard_map/ppermute | solution.py:51
  140.3 13.2 %collective-permute-start.16 = (f32[21,8,8,1]{0,2,3,1:T(8,128)S(1)}, f32[21,8,8,1]{0,2,3,1:T(8,128)S(1)}, u32[]{:S(2)}, u32[]{:S(2)}) collective-permute-start(f32[21,8,8,1]{0,2,3,1:T(8,128)S(1)} %copy.52), channel_id=1, source_target_pairs={{0,16},{16,32},{32,48},{48,64},{64,80},{80,96},{96,112},{112,128},... | collective-permute-start | bytes 16136 | tf_op jit(solution)/shard_map/ppermute | solution.py:48
  141.5 12.8 %collective-permute-start.17 = (f32[21,8,8,1]{0,2,3,1:T(8,128)S(1)}, f32[21,8,8,1]{0,2,3,1:T(8,128)S(1)}, u32[]{:S(2)}, u32[]{:S(2)}) collective-permute-start(f32[21,8,8,1]{0,2,3,1:T(8,128)S(1)} %copy.54), channel_id=1, source_target_pairs={{16,0},{32,16},{48,32},{64,48},{80,64},{96,80},{112,96},{128,112},... | collective-permute-start | bytes 16136 | tf_op jit(solution)/shard_map/ppermute | solution.py:51
  146.2 21.8 %collective-permute-start.22 = (f32[1,8,1,130]{3,2,1,0:T(1,128)}, f32[1,8,1,130]{3,2,1,0:T(1,128)}, u32[]{:S(2)}, u32[]{:S(2)}) collective-permute-start(f32[1,8,1,130]{3,2,1,0:T(1,128)} %get-tuple-element.428), channel_id=1, source_target_pairs={{1,0},{2,1},{3,2},{4,3},{5,4},{6,5},{7,6},{8,7},{9,8},{10,9},{11,1... | collective-permute-start | bytes 12488 | tf_op jit(solution)/shard_map/ppermute | solution.py:51
  151.4 16.7 %collective-permute-start.23 = (f32[1,8,1,130]{3,2,1,0:T(1,128)}, f32[1,8,1,130]{3,2,1,0:T(1,128)}, u32[]{:S(2)}, u32[]{:S(2)}) collective-permute-start(f32[1,8,1,130]{3,2,1,0:T(1,128)} %get-tuple-element.429), channel_id=1, source_target_pairs={{0,1},{1,2},{2,3},{3,4},{4,5},{5,6},{6,7},{7,8},{8,9},{9,10},{10,1... | collective-permute-start | bytes 12488 | tf_op jit(solution)/shard_map/ppermute | solution.py:48
  156.4 7.7 %collective-permute-start.18 = (f32[21,8,1,130]{3,2,1,0:T(1,128)S(1)}, f32[21,8,1,130]{3,2,1,0:T(1,128)S(1)}, u32[]{:S(2)}, u32[]{:S(2)}) collective-permute-start(f32[21,8,1,130]{3,2,1,0:T(1,128)S(1)} %get-tuple-element.329), channel_id=1, source_target_pairs={{0,1},{1,2},{2,3},{3,4},{4,5},{5,6},{6,7},{7,8},{8,9},{9,10},{10,1... | collective-permute-start | bytes 262088 | tf_op jit(solution)/shard_map/ppermute | solution.py:48
  156.5 7.6 %collective-permute-start.19 = (f32[21,8,1,130]{3,2,1,0:T(1,128)S(1)}, f32[21,8,1,130]{3,2,1,0:T(1,128)S(1)}, u32[]{:S(2)}, u32[]{:S(2)}) collective-permute-start(f32[21,8,1,130]{3,2,1,0:T(1,128)S(1)} %get-tuple-element.328), channel_id=1, source_target_pairs={{1,0},{2,1},{3,2},{4,3},{5,4},{6,5},{7,6},{8,7},{9,8},{10,9},{11,1... | collective-permute-start | bytes 262088 | tf_op jit(solution)/shard_map/ppermute | solution.py:51
  170.0 14.1 %collective-permute-start.24 = (f32[2,8,8,1]{3,0,2,1:T(2,128)S(1)}, f32[2,8,8,1]{3,0,2,1:T(2,128)S(1)}, u32[]{:S(2)}, u32[]{:S(2)}) collective-permute-start(f32[2,8,8,1]{3,0,2,1:T(2,128)S(1)} %get-tuple-element.502), channel_id=1, source_target_pairs={{0,16},{16,32},{32,48},{48,64},{64,80},{80,96},{96,112},{112,128},... | collective-permute-start | bytes 1544 | tf_op jit(solution)/shard_map/ppermute | solution.py:48
  170.8 13.4 %collective-permute-start.25 = (f32[2,8,8,1]{3,0,2,1:T(2,128)S(1)}, f32[2,8,8,1]{3,0,2,1:T(2,128)S(1)}, u32[]{:S(2)}, u32[]{:S(2)}) collective-permute-start(f32[2,8,8,1]{3,0,2,1:T(2,128)S(1)} %get-tuple-element.501), channel_id=1, source_target_pairs={{16,0},{32,16},{48,32},{64,48},{80,64},{96,80},{112,96},{128,112},... | collective-permute-start | bytes 1544 | tf_op jit(solution)/shard_map/ppermute | solution.py:51
  214.5 6.2 %collective-permute-start.35 = (f32[2,8,1,130]{3,0,2,1:T(2,128)S(1)}, f32[2,8,1,130]{3,0,2,1:T(2,128)S(1)}, u32[]{:S(2)}, u32[]{:S(2)}) collective-permute-start(f32[2,8,1,130]{3,0,2,1:T(2,128)S(1)} %get-tuple-element.397), channel_id=1, source_target_pairs={{0,1},{1,2},{2,3},{3,4},{4,5},{5,6},{6,7},{7,8},{8,9},{9,10},{10,1... | collective-permute-start | bytes 24968 | tf_op jit(solution)/shard_map/ppermute | solution.py:48
  (307 other events, 840.9 us)
where the time goes:
time: 488 us; the launch traced here: 479 us
  blocking collectives  156 us (32%)
  starting transfers between devices  104 us (21%)
  other arithmetic  70.3 us (14%)
  waiting for transfers between devices  55.8 us (11%)
  local copies, waits for them, and re-layouts  50.7 us (10%)
  between operations  25.1 us (5%)
  matrix products  17.1 us (4%)
    psum x2, blocking collectives, local(): gram_matrix = lax.psum(local_gram, ('gx', 'gy'))  156 us
    ppermute x28, starting transfers between devices, padded_2(): lax.ppermute(lax.slice_in_dim(block, 0, width, axis=dim), axis, backward)  80.6 us
    unnamed x81, other arithmetic  41.9 us
    ppermute x28, waiting for transfers between devices, padded_2(): lax.ppermute(lax.slice_in_dim(block, block.shape[dim] - width, None, axis...  41.5 us
    ppermute x28, starting transfers between devices, padded_2(): lax.ppermute(lax.slice_in_dim(block, block.shape[dim] - width, None, axis...  23 us
    unnamed x538, local copies, waits for them, and re-layouts  22.3 us
    ppermute x28, waiting for transfers between devices, padded_2(): lax.ppermute(lax.slice_in_dim(block, 0, width, axis=dim), axis, backward)  14.2 us
  transfers between devices with their start and end apart: 56, of which 35 were waited for; matrix products, arithmetic and copies ran while one was open for 18% of the time, Pallas kernels for 0%

commit v1 on v0

--- a/solution.py
+++ b/solution.py
@@ -303,7 +303,8 @@
                 r_levels.append(current[1])
         basis = jnp.stack(p_levels + r_levels)
         local_gram = jnp.einsum("aijk,bijk->ab", basis, basis, precision=highest)
-        gram_matrix = lax.psum(local_gram, ("gx", "gy"))
+        partial = lax.psum(local_gram, "gy")
+        gram_matrix = lax.psum(partial, "gx")
         sol_co, resid_co, search_co = krylov_steps(gram_matrix)
         solution = solution + jnp.tensordot(sol_co, basis, axes=1, precision=highest)
         residual = jnp.tensordot(resid_co, basis, axes=1, precision=highest)

time: 488 us -> 459 us (0.941)
  blocking collectives: 156 us -> 128 us
    psum x2 -> x4, blocking collectives: 156 us -> 128 us  [the longest x2 69.8 us: local(): gram_matrix = lax.psum(partial, 'gx')]
  transfers between devices with their start and end apart: 56 -> 56, of which waited for: 35 -> 35; matrix products, arithmetic and copies ran while one was open for 18% -> 20% of each run, Pallas kernels for 0% -> 0%
where the time goes in v1:
time: 459 us; the launch traced here: 450 us
  blocking collectives  128 us (28%)
  starting transfers between devices  104 us (23%)
  other arithmetic  70.3 us (15%)
  waiting for transfers between devices  55.9 us (12%)
  local copies, waits for them, and re-layouts  50.6 us (11%)
  between operations  24.3 us (5%)
  matrix products  16.6 us (4%)
    ppermute x28, starting transfers between devices, padded_2(): lax.ppermute(lax.slice_in_dim(block, 0, width, axis=dim), axis, backward)  81.3 us
    psum x2, blocking collectives, local(): gram_matrix = lax.psum(partial, 'gx')  69.8 us
    psum x2, blocking collectives, local(): partial = lax.psum(local_gram, 'gy')  58.6 us
    ppermute x28, waiting for transfers between devices, padded_2(): lax.ppermute(lax.slice_in_dim(block, block.shape[dim] - width, None, axis...  42.1 us
    unnamed x81, other arithmetic  41.9 us
    ppermute x28, starting transfers between devices, padded_2(): lax.ppermute(lax.slice_in_dim(block, block.shape[dim] - width, None, axis...  22.7 us
    unnamed x538, local copies, waits for them, and re-layouts  22.3 us
    ppermute x28, waiting for transfers between devices, padded_2(): lax.ppermute(lax.slice_in_dim(block, 0, width, axis=dim), axis, backward)  13.8 us
  transfers between devices with their start and end apart: 56, of which 35 were waited for; matrix products, arithmetic and copies ran while one was open for 20% of the time, Pallas kernels for 0%

profile of v1, /device:TPU:1, one launch (start us, length us, event | category | flops | bytes accessed | tf_op | source)
XLA Modules:
  0.0 450.2 jit_solution(2203528703605491214)
XLA Ops:
  11.4 3.8 collective-permute-start.3
  32.1 3.3 collective-permute-start.5
  43.5 5.4 %collective-permute-start.7 = (f32[21,8,1,130]{3,2,1,0:T(1,128)S(1)}, f32[21,8,1,130]{3,2,1,0:T(1,128)S(1)}, u32[]{:S(2)}, u32[]{:S(2)}) collective-permute-start(f32[21,8,1,130]{3,2,1,0:T(1,128)S(1)} %get-tuple-element.347), channel_id=1, source_target_pairs={{1,0},{2,1},{3,2},{4,3},{5,4},{6,5},{7,6},{8,7},{9,8},{10,9},{11,1... | collective-permute-start | bytes 262088 | tf_op jit(solution)/shard_map/ppermute | solution.py:51
  79.4 5.8 %collective-permute-start.11 = (f32[21,8,1,130]{3,2,1,0:T(1,128)S(1)}, f32[21,8,1,130]{3,2,1,0:T(1,128)S(1)}, u32[]{:S(2)}, u32[]{:S(2)}) collective-permute-start(f32[21,8,1,130]{3,2,1,0:T(1,128)S(1)} %get-tuple-element.341), channel_id=1, source_target_pairs={{1,0},{2,1},{3,2},{4,3},{5,4},{6,5},{7,6},{8,7},{9,8},{10,9},{11,1... | collective-permute-start | bytes 262088 | tf_op jit(solution)/shard_map/ppermute | solution.py:51
  115.1 5.6 %collective-permute-start.15 = (f32[21,8,1,130]{3,2,1,0:T(1,128)S(1)}, f32[21,8,1,130]{3,2,1,0:T(1,128)S(1)}, u32[]{:S(2)}, u32[]{:S(2)}) collective-permute-start(f32[21,8,1,130]{3,2,1,0:T(1,128)S(1)} %get-tuple-element.335), channel_id=1, source_target_pairs={{1,0},{2,1},{3,2},{4,3},{5,4},{6,5},{7,6},{8,7},{9,8},{10,9},{11,1... | collective-permute-start | bytes 262088 | tf_op jit(solution)/shard_map/ppermute | solution.py:51
  141.4 3.2 collective-permute-start.17
  146.2 5.1 %collective-permute-start.22 = (f32[1,8,1,130]{3,2,1,0:T(1,128)}, f32[1,8,1,130]{3,2,1,0:T(1,128)}, u32[]{:S(2)}, u32[]{:S(2)}) collective-permute-start(f32[1,8,1,130]{3,2,1,0:T(1,128)} %get-tuple-element.428), channel_id=1, source_target_pairs={{1,0},{2,1},{3,2},{4,3},{5,4},{6,5},{7,6},{8,7},{9,8},{10,9},{11,1... | collective-permute-start | bytes 12488 | tf_op jit(solution)/shard_map/ppermute | solution.py:51
  156.5 4.8 %collective-permute-start.19 = (f32[21,8,1,130]{3,2,1,0:T(1,128)S(1)}, f32[21,8,1,130]{3,2,1,0:T(1,128)S(1)}, u32[]{:S(2)}, u32[]{:S(2)}) collective-permute-start(f32[21,8,1,130]{3,2,1,0:T(1,128)S(1)} %get-tuple-element.328), channel_id=1, source_target_pairs={{1,0},{2,1},{3,2},{4,3},{5,4},{6,5},{7,6},{8,7},{9,8},{10,9},{11,1... | collective-permute-start | bytes 262088 | tf_op jit(solution)/shard_map/ppermute | solution.py:51
  170.7 3.6 collective-permute-start.25
  184.2 5.2 %collective-permute-start.26 = (f32[2,8,1,130]{3,0,2,1:T(2,128)S(1)}, f32[2,8,1,130]{3,0,2,1:T(2,128)S(1)}, u32[]{:S(2)}, u32[]{:S(2)}) collective-permute-start(f32[2,8,1,130]{3,0,2,1:T(2,128)S(1)} %get-tuple-element.402), channel_id=1, source_target_pairs={{1,0},{2,1},{3,2},{4,3},{5,4},{6,5},{7,6},{8,7},{9,8},{10,9},{11,1... | collective-permute-start | bytes 24968 | tf_op jit(solution)/shard_map/ppermute | solution.py:51
  190.3 5.0 %collective-permute-done.27 = f32[2,8,1,130]{3,0,2,1:T(2,128)S(1)} collective-permute-done((f32[2,8,1,130]{3,0,2,1:T(2,128)S(1)}, f32[2,8,1,130]{3,0,2,1:T(2,128)S(1)}, u32[]{:S(2)}, u32[]{:S(2)}) %collective-permute-start.27) | collective-permute-done | bytes 8352 | tf_op jit(solution)/shard_map/ppermute | solution.py:48
  196.1 4.4 collective-permute-start.29
  208.2 5.1 %collective-permute-start.33 = (f32[2,8,8,1]{3,0,2,1:T(2,128)S(1)}, f32[2,8,8,1]{3,0,2,1:T(2,128)S(1)}, u32[]{:S(2)}, u32[]{:S(2)}) collective-permute-start(f32[2,8,8,1]{3,0,2,1:T(2,128)S(1)} %get-tuple-element.487), channel_id=1, source_target_pairs={{16,0},{32,16},{48,32},{64,48},{80,64},{96,80},{112,96},{128,112},... | collective-permute-start | bytes 1544 | tf_op jit(solution)/shard_map/ppermute | solution.py:51
  217.3 3.3 collective-permute-done.35
  221.3 5.1 %collective-permute-start.37 = (f32[1,8,8,1]{3,0,2,1:T(1,128)S(1)}, f32[1,8,8,1]{3,0,2,1:T(1,128)S(1)}, u32[]{:S(2)}, u32[]{:S(2)}) collective-permute-start(f32[1,8,8,1]{3,0,2,1:T(1,128)S(1)} %get-tuple-element.481), channel_id=1, source_target_pairs={{16,0},{32,16},{48,32},{64,48},{80,64},{96,80},{112,96},{128,112},... | collective-permute-start | bytes 776 | tf_op jit(solution)/shard_map/ppermute | solution.py:51
  235.1 29.3 %psum.28 = f32[9,9]{1,0:T(8,128)S(1)} all-reduce(f32[9,9]{1,0:T(8,128)S(1)} %convolution_bitcast_fusion.1), channel_id=1, replica_groups=mesh['gx'=16,'gy'=16] {'gy'}, use_global_device_ids=true, to_apply=%region_0.1 | all-reduce | flops 81 | bytes 648 | tf_op jit(solution)/shard_map/psum | solution.py:306
  264.4 34.9 %psum.29 = f32[9,9]{1,0:T(8,128)S(1)} all-reduce(f32[9,9]{1,0:T(8,128)S(1)} %psum.28), channel_id=1, replica_groups=mesh['gx'=16,'gy'=16] {'gx'}, use_global_device_ids=true, to_apply=%region_1.2 | all-reduce | flops 81 | bytes 648 | tf_op jit(solution)/shard_map/psum | solution.py:307
  325.4 4.8 %collective-permute-done.43 = f32[2,8,1,130]{3,0,2,1:T(2,128)S(1)} collective-permute-done((f32[2,8,1,130]{3,0,2,1:T(2,128)S(1)}, f32[2,8,1,130]{3,0,2,1:T(2,128)S(1)}, u32[]{:S(2)}, u32[]{:S(2)}) %collective-permute-start.43) | collective-permute-done | bytes 8352 | tf_op jit(solution)/shard_map/ppermute | solution.py:48
  338.8 3.4 collective-permute-done.47
  343.9 3.1 collective-permute-start.49
  351.0 3.4 collective-permute-done.51
  355.9 4.3 collective-permute-start.53
  368.8 29.4 %psum.30 = f32[9,9]{1,0:T(8,128)S(1)} all-reduce(f32[9,9]{1,0:T(8,128)S(1)} %convolution_bitcast_fusion), channel_id=1, replica_groups=mesh['gx'=16,'gy'=16] {'gy'}, use_global_device_ids=true, to_apply=%region_2.3 | all-reduce | flops 81 | bytes 648 | tf_op jit(solution)/shard_map/psum | solution.py:306
  398.1 34.9 %psum.31 = f32[9,9]{1,0:T(8,128)S(1)} all-reduce(f32[9,9]{1,0:T(8,128)S(1)} %psum.30), channel_id=1, replica_groups=mesh['gx'=16,'gy'=16] {'gx'}, use_global_device_ids=true, to_apply=%region_3.4 | all-reduce | flops 81 | bytes 648 | tf_op jit(solution)/shard_map/psum | solution.py:307
  (950 shorter events, 209.5 us)
Async XLA Ops:
  2.4 7.5 %collective-permute-start = (f32[2,8,8,1]{3,2,1,0:T(8,128)S(1)}, f32[2,8,8,1]{3,2,1,0:T(8,128)S(1)}, u32[]{:S(2)}, u32[]{:S(2)}) collective-permute-start(f32[2,8,8,1]{3,2,1,0:T(8,128)S(1)} %get-tuple-element.495), channel_id=1, source_target_pairs={{0,16},{16,32},{32,48},{48,64},{64,80},{80,96},{96,112},{112,128},... | collective-permute-start | bytes 1544 | tf_op jit(solution)/shard_map/ppermute | solution.py:48
  6.4 138.2 %collective-permute-start.20 = (f32[1,8,8,1]{3,2,1,0:T(8,128)}, f32[1,8,8,1]{3,2,1,0:T(8,128)}, u32[]{:S(2)}, u32[]{:S(2)}) collective-permute-start(f32[1,8,8,1]{3,2,1,0:T(8,128)} %get-tuple-element.508), channel_id=1, source_target_pairs={{0,16},{16,32},{32,48},{48,64},{64,80},{80,96},{96,112},{112,128},... | collective-permute-start | bytes 776 | tf_op jit(solution)/shard_map/ppermute | solution.py:48
  7.9 136.7 %collective-permute-start.21 = (f32[1,8,8,1]{3,2,1,0:T(8,128)}, f32[1,8,8,1]{3,2,1,0:T(8,128)}, u32[]{:S(2)}, u32[]{:S(2)}) collective-permute-start(f32[1,8,8,1]{3,2,1,0:T(8,128)} %get-tuple-element.507), channel_id=1, source_target_pairs={{16,0},{32,16},{48,32},{64,48},{80,64},{96,80},{112,96},{128,112},... | collective-permute-start | bytes 776 | tf_op jit(solution)/shard_map/ppermute | solution.py:51
  30.9 8.9 %collective-permute-start.4 = (f32[21,8,8,1]{0,2,3,1:T(8,128)S(1)}, f32[21,8,8,1]{0,2,3,1:T(8,128)S(1)}, u32[]{:S(2)}, u32[]{:S(2)}) collective-permute-start(f32[21,8,8,1]{0,2,3,1:T(8,128)S(1)} %copy.34), channel_id=1, source_target_pairs={{0,16},{16,32},{32,48},{48,64},{64,80},{80,96},{96,112},{112,128},... | collective-permute-start | bytes 16136 | tf_op jit(solution)/shard_map/ppermute | solution.py:48
  32.1 8.4 %collective-permute-start.5 = (f32[21,8,8,1]{0,2,3,1:T(8,128)S(1)}, f32[21,8,8,1]{0,2,3,1:T(8,128)}, u32[]{:S(2)}, u32[]{:S(2)}) collective-permute-start(f32[21,8,8,1]{0,2,3,1:T(8,128)S(1)} %copy.36), channel_id=1, source_target_pairs={{16,0},{32,16},{48,32},{64,48},{80,64},{96,80},{112,96},{128,112},... | collective-permute-start | bytes 16136 | tf_op jit(solution)/shard_map/ppermute | solution.py:51
  43.4 7.9 %collective-permute-start.6 = (f32[21,8,1,130]{3,2,1,0:T(1,128)S(1)}, f32[21,8,1,130]{3,2,1,0:T(1,128)S(1)}, u32[]{:S(2)}, u32[]{:S(2)}) collective-permute-start(f32[21,8,1,130]{3,2,1,0:T(1,128)S(1)} %get-tuple-element.346), channel_id=1, source_target_pairs={{0,1},{1,2},{2,3},{3,4},{4,5},{5,6},{6,7},{7,8},{8,9},{9,10},{10,1... | collective-permute-start | bytes 262088 | tf_op jit(solution)/shard_map/ppermute | solution.py:48
  43.5 7.8 %collective-permute-start.7 = (f32[21,8,1,130]{3,2,1,0:T(1,128)S(1)}, f32[21,8,1,130]{3,2,1,0:T(1,128)S(1)}, u32[]{:S(2)}, u32[]{:S(2)}) collective-permute-start(f32[21,8,1,130]{3,2,1,0:T(1,128)S(1)} %get-tuple-element.347), channel_id=1, source_target_pairs={{1,0},{2,1},{3,2},{4,3},{5,4},{6,5},{7,6},{8,7},{9,8},{10,9},{11,1... | collective-permute-start | bytes 262088 | tf_op jit(solution)/shard_map/ppermute | solution.py:51
  69.0 7.4 %collective-permute-start.8 = (f32[21,8,8,1]{0,2,3,1:T(8,128)S(1)}, f32[21,8,8,1]{0,2,3,1:T(8,128)S(1)}, u32[]{:S(2)}, u32[]{:S(2)}) collective-permute-start(f32[21,8,8,1]{0,2,3,1:T(8,128)S(1)} %copy.40), channel_id=1, source_target_pairs={{0,16},{16,32},{32,48},{48,64},{64,80},{80,96},{96,112},{112,128},... | collective-permute-start | bytes 16136 | tf_op jit(solution)/shard_map/ppermute | solution.py:48
  70.3 6.9 %collective-permute-start.9 = (f32[21,8,8,1]{0,2,3,1:T(8,128)S(1)}, f32[21,8,8,1]{0,2,3,1:T(8,128)S(1)}, u32[]{:S(2)}, u32[]{:S(2)}) collective-permute-start(f32[21,8,8,1]{0,2,3,1:T(8,128)S(1)} %copy.42), channel_id=1, source_target_pairs={{16,0},{32,16},{48,32},{64,48},{80,64},{96,80},{112,96},{128,112},... | collective-permute-start | bytes 16136 | tf_op jit(solution)/shard_map/ppermute | solution.py:51
  79.3 8.2 %collective-permute-start.10 = (f32[21,8,1,130]{3,2,1,0:T(1,128)S(1)}, f32[21,8,1,130]{3,2,1,0:T(1,128)S(1)}, u32[]{:S(2)}, u32[]{:S(2)}) collective-permute-start(f32[21,8,1,130]{3,2,1,0:T(1,128)S(1)} %get-tuple-element.340), channel_id=1, source_target_pairs={{0,1},{1,2},{2,3},{3,4},{4,5},{5,6},{6,7},{7,8},{8,9},{9,10},{10,1... | collective-permute-start | bytes 262088 | tf_op jit(solution)/shard_map/ppermute | solution.py:48
  79.4 8.2 %collective-permute-start.11 = (f32[21,8,1,130]{3,2,1,0:T(1,128)S(1)}, f32[21,8,1,130]{3,2,1,0:T(1,128)S(1)}, u32[]{:S(2)}, u32[]{:S(2)}) collective-permute-start(f32[21,8,1,130]{3,2,1,0:T(1,128)S(1)} %get-tuple-element.341), channel_id=1, source_target_pairs={{1,0},{2,1},{3,2},{4,3},{5,4},{6,5},{7,6},{8,7},{9,8},{10,9},{11,1... | collective-permute-start | bytes 262088 | tf_op jit(solution)/shard_map/ppermute | solution.py:51
  104.7 7.4 %collective-permute-start.12 = (f32[21,8,8,1]{0,2,3,1:T(8,128)S(1)}, f32[21,8,8,1]{0,2,3,1:T(8,128)S(1)}, u32[]{:S(2)}, u32[]{:S(2)}) collective-permute-start(f32[21,8,8,1]{0,2,3,1:T(8,128)S(1)} %copy.46), channel_id=1, source_target_pairs={{0,16},{16,32},{32,48},{48,64},{64,80},{80,96},{96,112},{112,128},... | collective-permute-start | bytes 16136 | tf_op jit(solution)/shard_map/ppermute | solution.py:48
  106.0 6.9 %collective-permute-start.13 = (f32[21,8,8,1]{0,2,3,1:T(8,128)S(1)}, f32[21,8,8,1]{0,2,3,1:T(8,128)S(1)}, u32[]{:S(2)}, u32[]{:S(2)}) collective-permute-start(f32[21,8,8,1]{0,2,3,1:T(8,128)S(1)} %copy.48), channel_id=1, source_target_pairs={{16,0},{32,16},{48,32},{64,48},{80,64},{96,80},{112,96},{128,112},... | collective-permute-start | bytes 16136 | tf_op jit(solution)/shard_map/ppermute | solution.py:51
  115.0 8.4 %collective-permute-start.14 = (f32[21,8,1,130]{3,2,1,0:T(1,128)S(1)}, f32[21,8,1,130]{3,2,1,0:T(1,128)S(1)}, u32[]{:S(2)}, u32[]{:S(2)}) collective-permute-start(f32[21,8,1,130]{3,2,1,0:T(1,128)S(1)} %get-tuple-element.334), channel_id=1, source_target_pairs={{0,1},{1,2},{2,3},{3,4},{4,5},{5,6},{6,7},{7,8},{8,9},{9,10},{10,1... | collective-permute-start | bytes 262088 | tf_op jit(solution)/shard_map/ppermute | solution.py:48
  115.1 8.3 %collective-permute-start.15 = (f32[21,8,1,130]{3,2,1,0:T(1,128)S(1)}, f32[21,8,1,130]{3,2,1,0:T(1,128)S(1)}, u32[]{:S(2)}, u32[]{:S(2)}) collective-permute-start(f32[21,8,1,130]{3,2,1,0:T(1,128)S(1)} %get-tuple-element.335), channel_id=1, source_target_pairs={{1,0},{2,1},{3,2},{4,3},{5,4},{6,5},{7,6},{8,7},{9,8},{10,9},{11,1... | collective-permute-start | bytes 262088 | tf_op jit(solution)/shard_map/ppermute | solution.py:51
  140.2 13.3 %collective-permute-start.16 = (f32[21,8,8,1]{0,2,3,1:T(8,128)S(1)}, f32[21,8,8,1]{0,2,3,1:T(8,128)S(1)}, u32[]{:S(2)}, u32[]{:S(2)}) collective-permute-start(f32[21,8,8,1]{0,2,3,1:T(8,128)S(1)} %copy.52), channel_id=1, source_target_pairs={{0,16},{16,32},{32,48},{48,64},{64,80},{80,96},{96,112},{112,128},... | collective-permute-start | bytes 16136 | tf_op jit(solution)/shard_map/ppermute | solution.py:48
  141.4 12.8 %collective-permute-start.17 = (f32[21,8,8,1]{0,2,3,1:T(8,128)S(1)}, f32[21,8,8,1]{0,2,3,1:T(8,128)S(1)}, u32[]{:S(2)}, u32[]{:S(2)}) collective-permute-start(f32[21,8,8,1]{0,2,3,1:T(8,128)S(1)} %copy.54), channel_id=1, source_target_pairs={{16,0},{32,16},{48,32},{64,48},{80,64},{96,80},{112,96},{128,112},... | collective-permute-start | bytes 16136 | tf_op jit(solution)/shard_map/ppermute | solution.py:51
  146.2 21.8 %collective-permute-start.22 = (f32[1,8,1,130]{3,2,1,0:T(1,128)}, f32[1,8,1,130]{3,2,1,0:T(1,128)}, u32[]{:S(2)}, u32[]{:S(2)}) collective-permute-start(f32[1,8,1,130]{3,2,1,0:T(1,128)} %get-tuple-element.428), channel_id=1, source_target_pairs={{1,0},{2,1},{3,2},{4,3},{5,4},{6,5},{7,6},{8,7},{9,8},{10,9},{11,1... | collective-permute-start | bytes 12488 | tf_op jit(solution)/shard_map/ppermute | solution.py:51
  151.3 16.7 %collective-permute-start.23 = (f32[1,8,1,130]{3,2,1,0:T(1,128)}, f32[1,8,1,130]{3,2,1,0:T(1,128)}, u32[]{:S(2)}, u32[]{:S(2)}) collective-permute-start(f32[1,8,1,130]{3,2,1,0:T(1,128)} %get-tuple-element.429), channel_id=1, source_target_pairs={{0,1},{1,2},{2,3},{3,4},{4,5},{5,6},{6,7},{7,8},{8,9},{9,10},{10,1... | collective-permute-start | bytes 12488 | tf_op jit(solution)/shard_map/ppermute | solution.py:48
  156.4 7.7 %collective-permute-start.18 = (f32[21,8,1,130]{3,2,1,0:T(1,128)S(1)}, f32[21,8,1,130]{3,2,1,0:T(1,128)S(1)}, u32[]{:S(2)}, u32[]{:S(2)}) collective-permute-start(f32[21,8,1,130]{3,2,1,0:T(1,128)S(1)} %get-tuple-element.329), channel_id=1, source_target_pairs={{0,1},{1,2},{2,3},{3,4},{4,5},{5,6},{6,7},{7,8},{8,9},{9,10},{10,1... | collective-permute-start | bytes 262088 | tf_op jit(solution)/shard_map/ppermute | solution.py:48
  156.5 7.6 %collective-permute-start.19 = (f32[21,8,1,130]{3,2,1,0:T(1,128)S(1)}, f32[21,8,1,130]{3,2,1,0:T(1,128)S(1)}, u32[]{:S(2)}, u32[]{:S(2)}) collective-permute-start(f32[21,8,1,130]{3,2,1,0:T(1,128)S(1)} %get-tuple-element.328), channel_id=1, source_target_pairs={{1,0},{2,1},{3,2},{4,3},{5,4},{6,5},{7,6},{8,7},{9,8},{10,9},{11,1... | collective-permute-start | bytes 262088 | tf_op jit(solution)/shard_map/ppermute | solution.py:51
  169.9 14.1 %collective-permute-start.24 = (f32[2,8,8,1]{3,0,2,1:T(2,128)S(1)}, f32[2,8,8,1]{3,0,2,1:T(2,128)S(1)}, u32[]{:S(2)}, u32[]{:S(2)}) collective-permute-start(f32[2,8,8,1]{3,0,2,1:T(2,128)S(1)} %get-tuple-element.502), channel_id=1, source_target_pairs={{0,16},{16,32},{32,48},{48,64},{64,80},{80,96},{96,112},{112,128},... | collective-permute-start | bytes 1544 | tf_op jit(solution)/shard_map/ppermute | solution.py:48
  170.7 13.3 %collective-permute-start.25 = (f32[2,8,8,1]{3,0,2,1:T(2,128)S(1)}, f32[2,8,8,1]{3,0,2,1:T(2,128)S(1)}, u32[]{:S(2)}, u32[]{:S(2)}) collective-permute-start(f32[2,8,8,1]{3,0,2,1:T(2,128)S(1)} %get-tuple-element.501), channel_id=1, source_target_pairs={{16,0},{32,16},{48,32},{64,48},{80,64},{96,80},{112,96},{128,112},... | collective-permute-start | bytes 1544 | tf_op jit(solution)/shard_map/ppermute | solution.py:51
  348.2 6.2 %collective-permute-start.51 = (f32[2,8,1,130]{3,0,2,1:T(2,128)S(1)}, f32[2,8,1,130]{3,0,2,1:T(2,128)S(1)}, u32[]{:S(2)}, u32[]{:S(2)}) collective-permute-start(f32[2,8,1,130]{3,0,2,1:T(2,128)S(1)} %get-tuple-element.391), channel_id=1, source_target_pairs={{0,1},{1,2},{2,3},{3,4},{4,5},{5,6},{6,7},{7,8},{8,9},{9,10},{10,1... | collective-permute-start | bytes 24968 | tf_op jit(solution)/shard_map/ppermute | solution.py:48
  (307 other events, 753.2 us)
